TPU v7x, 32 devices: a whole 2x2x4 slice. The times are simulated.
32 devices in a mesh: rollout: 2 (over y), branch: 4 (over z), seq: 4 (over x, core).
Axes of the slice: x: 2, y: 2, z: 4, core: 2. Of those that a mesh axis runs over, the one named last changes fastest.
Arguments:
- queries: bfloat16 [8, 512, 4096], P(('rollout', 'branch'), 'seq'), parts along dimension 0, may hold values from -8 to 8
- keyvals: bfloat16 [8, 512, 2, 256], P(('rollout', 'branch'), 'seq'), parts along dimension 0, may hold values from -4 to 4
- residual: bfloat16 [8, 512, 4096], P(('rollout', 'branch'), 'seq'), parts along dimension 0, may hold values from -3 to 3
- read_list: int32 [8, 4, 3], P(('rollout', 'branch'), 'seq'), parts along dimension 0, may hold values from 0 to 3
- router: bfloat16 [4096, 8], replicated, may hold values from -0.09375 to 0.09375
- expert_ids: int32 [8, 512, 2], P(('rollout', 'branch'), 'seq'), parts along dimension 0, may hold values from 0 to 7, all different within a row; in each aligned block of 128 rows (0 to 127, 128 to 255, ..., all dimensions but the last counted through in order) at most 48 rows name the same one
- w_gate_up: bfloat16 [16, 4096, 2, 384], P(('branch', 'seq')), may hold values from -0.09375 to 0.09375
- w_down: bfloat16 [16, 384, 4096], P(('branch', 'seq')), may hold values from -0.21875 to 0.21875
Outputs:
- mixed: bfloat16 [8, 512, 4096], P(('rollout', 'branch'), 'seq'), parts along dimension 0
There are 2 independent parts, one for each index of `rollout`. A program takes and returns all parts, laid end to end along the dimension named above; an argument that names none is the same for every part. Nothing has to cross between parts.
Inputs may be any that keep to these rules, and one draw needn't show every extreme that they name: read_list[c, s, o] is the block of branch c that query block s of branch (c + o + 1) mod 4 reads. `expert_ids`: each token names 2 different experts; of the 128 tokens of one device at most 48 name one expert, and in every draw some expert is named by exactly 48 tokens of some device.
All inputs are finite; a program needn't handle non-finite values.
Results may differ from a plain program's by a relative error of at most 0.0062.
Values may be sent and summed in bfloat16 or wider, within the bound.
A program may use at most 192 MiB of HBM per device.

v0:
```python
import math
import jax
import jax.numpy as jnp
from jax import lax
from jax.sharding import PartitionSpec as P

D = 4096
HEAD_SIZE = 128
QUERY_HEADS = 32
KEY_VALUE_HEADS = 2


def swapped(value, axis, apart):
    mask = 2**apart
    pairs = [(source, source ^ mask) for source in range(lax.axis_size(axis))]
    return lax.ppermute(value, axis, pairs)


def attend_block(q_rows, own_kv, sib_kv, block_index):
    block_len = q_rows.shape[0]
    length_own = own_kv.shape[0]
    positions = block_index * block_len + jnp.arange(block_len, dtype=jnp.int32)
    own_allowed = jnp.arange(length_own, dtype=jnp.int32)[None, :] <= positions[:, None]
    allowed = jnp.concatenate(
        [own_allowed, jnp.ones((block_len, sib_kv.shape[0]), dtype=bool)], axis=1
    )
    key_rows = jnp.concatenate([own_kv[:, 0], sib_kv[:, 0]], axis=0)
    value_rows = jnp.concatenate([own_kv[:, 1], sib_kv[:, 1]], axis=0)
    group_count = QUERY_HEADS // KEY_VALUE_HEADS
    sub_heads = min(group_count, 8)
    inv_scale = 1.0 / math.sqrt(HEAD_SIZE)
    pieces = []
    for head_key_value in range(KEY_VALUE_HEADS):
        key_head = key_rows[:, head_key_value * HEAD_SIZE : (head_key_value + 1) * HEAD_SIZE]
        value_head = value_rows[:, head_key_value * HEAD_SIZE : (head_key_value + 1) * HEAD_SIZE]
        for start_head in range(0, group_count, sub_heads):
            column = (head_key_value * group_count + start_head) * HEAD_SIZE
            query_head = q_rows[:, column : column + sub_heads * HEAD_SIZE].reshape(
                block_len, sub_heads, HEAD_SIZE
            )
            raw_scores = jnp.einsum(
                "tgd,kd->gtk", query_head, key_head, preferred_element_type=jnp.float32
            )
            masked = jnp.where(allowed[None], raw_scores, -1e30)
            row_max = jnp.max(masked, axis=-1, keepdims=True) * inv_scale
            expterm = jnp.exp(masked * inv_scale - row_max)
            probs = (expterm / jnp.sum(expterm, axis=-1, keepdims=True)).astype(jnp.bfloat16)
            mixture = jnp.einsum(
                "gtk,kd->tgd", probs, value_head, preferred_element_type=jnp.float32
            )
            pieces.append(mixture.reshape(block_len, sub_heads * HEAD_SIZE).astype(jnp.bfloat16))
    return jnp.concatenate(pieces, axis=1)


def on_device(queries, keyvals, residual, read_list, router, expert_ids, w_gate_up, w_down):
    block_len = queries.shape[1]
    kv_width = keyvals.shape[-1]
    seq_blocks = lax.axis_size("seq")
    branches = lax.axis_size("branch")
    me_branch = lax.axis_index("branch")
    me_block = lax.axis_index("seq")
    suffix_all = lax.all_gather(keyvals, "seq", axis=1, tiled=True)[0]
    blocks = suffix_all.reshape(seq_blocks, block_len, 2, kv_width)
    picked = blocks[read_list[0, 0]]
    by_offset = jnp.concatenate(
        [jnp.zeros((1, block_len, 2, kv_width), keyvals.dtype), picked], axis=0
    )
    by_dest = (jnp.arange(branches, dtype=jnp.int32) - me_branch) % branches
    outgoing = by_offset[by_dest]
    incoming = lax.all_to_all(outgoing, "branch", split_axis=0, concat_axis=0, tiled=True)
    others = (me_branch + 1 + jnp.arange(branches - 1, dtype=jnp.int32)) % branches
    sibling = incoming[others].reshape((branches - 1) * block_len, 2, kv_width)
    context = attend_block(queries[0], suffix_all, sibling, me_block)
    state = residual[0].astype(jnp.float32) + context.astype(jnp.float32)
    normed = (state * lax.rsqrt(jnp.mean(state * state, axis=-1, keepdims=True) + 1e-06)).astype(
        jnp.bfloat16
    )
    logits = jnp.dot(normed, router, preferred_element_type=jnp.float32)
    routed = expert_ids[0]
    top_count = routed.shape[1]
    experts = router.shape[1]
    chosen_logits = jnp.take_along_axis(logits, routed, axis=1)
    gate_mix = 1.0 / jnp.sum(
        jnp.exp(chosen_logits[:, None, :] - chosen_logits[:, :, None]), axis=-1
    )
    capacity = 2 * ((3 * block_len * top_count + 4 * experts - 1) // (4 * experts))
    half_cap = capacity // 2
    flat_ids = routed.reshape(-1)
    onehot = (flat_ids[:, None] == jnp.arange(experts, dtype=jnp.int32)[None, :]).astype(jnp.int32)
    slot_of = jnp.sum((jnp.cumsum(onehot, axis=0) - 1) * onehot, axis=1)
    row_token = jnp.arange(block_len * top_count, dtype=jnp.int32) // top_count
    sendbuf = (
        jnp.zeros((experts, capacity, D), jnp.bfloat16).at[flat_ids, slot_of].set(normed[row_token])
    )
    pair_half = me_block % 2
    halved = sendbuf.reshape(experts * 2, half_cap, D)
    own_share = lax.all_to_all(halved, ("branch", "seq"), split_axis=0, concat_axis=0, tiled=True)
    theirs = swapped(own_share, "seq", 0)
    rows_in = jnp.where(
        pair_half == 0,
        jnp.concatenate([own_share, theirs], axis=1),
        jnp.concatenate([theirs, own_share], axis=1),
    )
    devices = rows_in.shape[0]
    half_width = D // 2
    expert_rows = rows_in.reshape(devices * capacity, D)
    gate_up = jnp.einsum(
        "rd,dcf->rcf", expert_rows, w_gate_up[0], preferred_element_type=jnp.float32
    )
    hidden_act = (jax.nn.silu(gate_up[:, 0]) * gate_up[:, 1]).astype(jnp.bfloat16)
    down_local = w_down[0]
    kept_cols = lax.dynamic_slice_in_dim(down_local, pair_half * half_width, half_width, 1)
    given_cols = lax.dynamic_slice_in_dim(down_local, (1 - pair_half) * half_width, half_width, 1)
    kept_share = jnp.dot(hidden_act, kept_cols, preferred_element_type=jnp.float32).reshape(
        devices, capacity, half_width
    )
    given_share = jnp.dot(hidden_act, given_cols, preferred_element_type=jnp.float32).reshape(
        devices, capacity, half_width
    )
    gotten = swapped(given_share, "seq", 0)
    finished = (kept_share + gotten).astype(jnp.bfloat16)
    returned = lax.all_to_all(finished, ("branch", "seq"), split_axis=0, concat_axis=0, tiled=True)
    out_table = jnp.swapaxes(returned.reshape(experts, 2, capacity, half_width), 1, 2).reshape(
        experts, capacity, D
    )
    expert_out = out_table[flat_ids, slot_of].reshape(block_len, top_count, D)
    layer_out = state
    for slot_k in range(top_count):
        layer_out = layer_out + gate_mix[:, slot_k : slot_k + 1] * expert_out[:, slot_k].astype(
            jnp.float32
        )
    return layer_out.astype(jnp.bfloat16)[None]


def solution(mesh):
    return jax.shard_map(
        on_device,
        mesh=mesh,
        in_specs=(
            P(("rollout", "branch"), "seq", None),
            P(("rollout", "branch"), "seq", None, None),
            P(("rollout", "branch"), "seq", None),
            P(("rollout", "branch"), "seq", None),
            P(),
            P(("rollout", "branch"), "seq", None),
            P(("branch", "seq"), None, None, None),
            P(("branch", "seq"), None, None),
        ),
        out_specs=P(("rollout", "branch"), "seq", None),
        check_vma=False,
    )
```

profile of v0, /device:TPU:11, one launch (start us, length us, event | category | flops | bytes accessed | tf_op | source)
XLA Modules:
  0.0 366.1 jit_solution(11561085254637891067)
XLA Ops:
  1.1 7.7 %all_gather.3 = bf16[1,512,2,256]{3,1,2,0:T(8,128)(2,1)} all-gather(bf16[1,128,2,256]{3,1,2,0:T(8,128)(2,1)S(1)} %copy.62), channel_id=1, replica_groups=mesh['rollout'=2,'branch'=4,'seq'=4] {'seq'}, dimensions={1}, use_global_device_ids=true | all-gather | bytes 655360 | tf_op jit(solution)/shard_map/all_gather | solution.py:62
  12.0 2.4 gather_fusion.1
  14.4 4.8 %all-to-all-start = ((bf16[4,128,2,256]{3,1,2,0:T(8,128)(2,1)}), bf16[4,128,2,256]{3,1,2,0:T(8,128)(2,1)}, u32[]{:S(2)}, u32[]{:S(2)}) async-start(bf16[4,128,2,256]{3,1,2,0:T(8,128)(2,1)} %gather_fusion.1), calls=%async_computation | async-start | bytes 1048576 | tf_op jit(solution)/shard_map/all_to_all | solution.py:70
  19.7 2.3 copy.64
  25.5 2.2 fusion.77
  27.7 2.7 all-to-all-done
  30.4 2.4 gather_fusion.2
  39.5 3.4 fusion.6
  42.9 1.8 fusion.26
  45.9 4.0 %fusion.25 = bf16[128,8,128]{2,0,1:T(8,128)(2,1)} fusion(f32[896,128,8]{1,0,2:T(8,128)} %copy-done.3, f32[8,128]{1,0:T(8,128)S(1)} %get-tuple-element.6, f32[8,128]{1,0:T(8,128)S(1)} %get-tuple-element.30, pred[128,896]{0,1:T(8,128)(4,1)} %concatenate.44, bf16[512,256]{1,0:T(8,128)(2,1)} %get-tuple-element.21, bf16[384,256]{1,0:T(8,128)(2,1)} %copy-done.14), kind=kOutput, calls=%fused_computation.52 | convolution fusion | flops 240058368 | bytes 4513792 | tf_op jit(solution)/shard_map/gtk,kd->tgd/dot_general | solution.py:48
  51.7 4.0 %fusion.24 = bf16[128,8,128]{2,0,1:T(8,128)(2,1)} fusion(f32[896,128,8]{1,0,2:T(8,128)} %copy-done.2, f32[8,128]{1,0:T(8,128)S(1)} %get-tuple-element.7, f32[8,128]{1,0:T(8,128)S(1)} %get-tuple-element.29, pred[128,896]{0,1:T(8,128)(4,1)} %concatenate.44, bf16[384,256]{1,0:T(8,128)(2,1)} %copy-done.14, bf16[512,256]{1,0:T(8,128)(2,1)} %get-tuple-element.21), kind=kOutput, calls=%fused_computation.51 | convolution fusion | flops 240058368 | bytes 4513792 | tf_op jit(solution)/shard_map/gtk,kd->tgd/dot_general | solution.py:48
  57.5 4.0 %fusion.23 = bf16[128,8,128]{2,0,1:T(8,128)(2,1)} fusion(f32[896,128,8]{1,0,2:T(8,128)} %copy-done.1, f32[8,128]{1,0:T(8,128)S(1)} %get-tuple-element.8, f32[8,128]{1,0:T(8,128)S(1)} %get-tuple-element.28, pred[128,896]{0,1:T(8,128)(4,1)} %concatenate.44, bf16[384,256]{1,0:T(8,128)(2,1)} %copy-done.14, bf16[512,256]{1,0:T(8,128)(2,1)} %get-tuple-element.21), kind=kOutput, calls=%fused_computation.50 | convolution fusion | flops 240058368 | bytes 4513792 | tf_op jit(solution)/shard_map/gtk,kd->tgd/dot_general | solution.py:48
  63.2 1.8 multiply_reduce_fusion
  65.1 2.8 multiply_convert_fusion
  67.9 6.6 %gather_fusion.3 = bf16[256,4096]{1,0:T(8,128)(2,1)} fusion(bf16[128,4096]{1,0:T(8,128)(2,1)} %multiply_convert_fusion, s32[1024]{0:T(1024)S(1)} %pad_clamp_fusion), kind=kCustom, calls=%fused_computation.3 | custom fusion | bytes 4195328 | tf_op jit(solution)/shard_map/gather | solution.py:93
  74.5 2.0 broadcast_in_dim.33
  76.5 66.6 %scatter_fusion = bf16[8,48,4096]{2,1,0:T(8,128)(2,1)} fusion(bf16[8,48,4096]{2,1,0:T(8,128)(2,1)} %broadcast_in_dim.33, s32[256]{0:T(256)S(1)} %bitcast.187, bf16[256,4096]{1,0:T(8,128)(2,1)} %gather_fusion.3), kind=kCustom, calls=%fused_computation.6 | custom fusion | bytes 6293504 | tf_op jit(solution)/shard_map/scatter | solution.py:93
  143.1 79.2 %all_to_all.15 = bf16[16,24,4096]{2,1,0:T(8,128)(2,1)} all-to-all(bf16[16,24,4096]{2,1,0:T(8,128)(2,1)} %bitcast.184), channel_id=1, replica_groups=mesh['rollout'=2,'branch'=4,'seq'=4] {'branch','seq'}, dimensions={0} | all-to-all | bytes 6291456 | tf_op jit(solution)/shard_map/all_to_all | solution.py:97
  222.5 5.9 %collective-permute-done = bf16[16,24,4096]{2,1,0:T(8,128)(2,1)} collective-permute-done((bf16[16,24,4096]{2,1,0:T(8,128)(2,1)}, bf16[16,24,4096]{2,1,0:T(8,128)(2,1)}, u32[]{:S(2)}, u32[]{:S(2)}) %collective-permute-start) | collective-permute-done | bytes 3145760 | tf_op jit(solution)/shard_map/ppermute | solution.py:16
  228.4 5.8 %maximum_select_fusion = bf16[16,48,4096]{2,1,0:T(8,128)(2,1)S(1)} fusion(bf16[16,24,4096]{2,1,0:T(8,128)(2,1)} %collective-permute-done, bf16[16,24,4096]{2,1,0:T(8,128)(2,1)} %all_to_all.15, pred[]{:T(512)S(6)} %eq.34), kind=kLoop, calls=%fused_computation.7 | loop fusion | flops 28311552 | bytes 12582913 | tf_op jit(solution)/shard_map/jit(_where)/select_n | solution.py:99
  234.2 7.3 %fusion = f32[768,2,384]{2,0,1:T(8,128)S(1)} fusion(bf16[768,4096,1]{1,0,2:T(8,128)(2,1)S(1)} %bitcast.190, bf16[4096,2,384]{2,1,0:T(2,128)(2,1)} %bitcast.209), kind=kOutput, calls=%fused_computation.8 | convolution fusion | flops 4831838208 | bytes 14942208 | tf_op jit(solution)/shard_map/rd,dcf->rcf/dot_general | solution.py:107
  241.9 4.5 %fusion.18 = f32[16,48,2048]{2,1,0:T(8,128)} fusion(bf16[16,48,384]{2,1,0:T(8,128)(2,1)S(1)} %bitcast.188, bf16[1,384,4096]{2,1,0:T(8,128)(2,1)S(1)} %copy-done, s32[]{:T(128)S(6)} %select_n.199), kind=kOutput, calls=%fused_computation.45 | convolution fusion | flops 1207959552 | bytes 8454148 | tf_op jit(solution)/shard_map/dot_general | solution.py:117
  246.5 10.4 %collective-permute-done.1 = f32[16,48,2048]{2,1,0:T(8,128)} collective-permute-done((f32[16,48,2048]{2,1,0:T(8,128)}, f32[16,48,2048]{2,1,0:T(8,128)}, u32[]{:S(2)}, u32[]{:S(2)}) %collective-permute-start.1) | collective-permute-done | bytes 6291488 | tf_op jit(solution)/shard_map/ppermute | solution.py:16
  256.8 6.5 %add_convert_fusion = bf16[16,48,2048]{2,1,0:T(8,128)(2,1)} fusion(f32[16,48,2048]{2,1,0:T(8,128)} %collective-permute-done.1, bf16[16,48,384]{2,1,0:T(8,128)(2,1)} %bitcast.189, bf16[1,384,4096]{2,1,0:T(8,128)(2,1)S(1)} %copy-done, s32[]{:T(128)S(6)} %select_n.198), kind=kOutput, calls=%fused_computation.10 | convolution fusion | flops 1211105280 | bytes 11599876 | tf_op jit(solution)/shard_map/dot_general | solution.py:114
  263.3 5.3 %all-to-all-start.2 = ((bf16[16,48,2048]{2,1,0:T(8,128)(2,1)}), bf16[16,48,2048]{2,1,0:T(8,128)(2,1)}, u32[]{:S(2)}, u32[]{:S(2)}) async-start(bf16[16,48,2048]{2,1,0:T(8,128)(2,1)} %add_convert_fusion), calls=%async_computation.2 | async-start | bytes 6291456 | tf_op jit(solution)/shard_map/all_to_all | solution.py:122
  275.0 1.8 copy.79
  278.7 59.8 %all-to-all-done.2 = bf16[16,48,2048]{2,1,0:T(8,128)(2,1)} async-done(((bf16[16,48,2048]{2,1,0:T(8,128)(2,1)}), bf16[16,48,2048]{2,1,0:T(8,128)(2,1)}, u32[]{:S(2)}, u32[]{:S(2)}) %all-to-all-start.2) | async-done | bytes 3145760 | tf_op jit(solution)/shard_map/all_to_all | solution.py:122
  338.5 4.0 %copy.114 = bf16[8,2,6,8,2048]{4,3,1,2,0:T(8,128)(2,1)} copy(bf16[8,2,6,8,2048]{4,3,2,1,0:T(8,128)(2,1)} %bitcast.75) | data formatting | bytes 6291456 | tf_op jit(solution)/shard_map/reshape | solution.py:123
  342.5 7.5 %gather_fusion.4 = bf16[256,4096]{1,0:T(8,128)(2,1)} fusion(bf16[8,48,4096]{2,1,0:T(8,128)(2,1)} %bitcast.185, s32[256]{0:T(256)S(1)} %bitcast.186), kind=kCustom, calls=%fused_computation.4 | custom fusion | bytes 4196352 | tf_op jit(solution)/shard_map/gather | solution.py:126
  350.0 4.4 %reshape.546 = bf16[128,2,4096]{2,1,0:T(2,128)(2,1)} reshape(bf16[256,4096]{1,0:T(8,128)(2,1)} %gather_fusion.4) | data formatting | bytes 4194304 | tf_op jit(solution)/shard_map/reshape | solution.py:126
  354.4 6.2 %fusion.76 = (bf16[128,1,4096]{2,1,0:T(2,128)(2,1)S(1)}, bf16[128,1,4096]{2,1,0:T(2,128)(2,1)S(1)}) fusion(bf16[128,2,4096]{2,1,0:T(2,128)(2,1)} %reshape.546), kind=kLoop, calls=%fused_computation.149 | loop fusion | bytes 4194304 | tf_op jit(solution)/shard_map/slice | solution.py:129
  360.7 5.2 %fusion.12 = bf16[1,128,4096]{2,1,0:T(8,128)(2,1)} fusion(bf16[1,128,4096]{2,1,0:T(8,128)(2,1)S(1)} %copy-done.4, bf16[1,128,1024]{2,1,0:T(8,128)(2,1)S(1)} %copy-done.9, bf16[1,128,1024]{2,1,0:T(8,128)(2,1)S(1)} %copy-done.8, bf16[1,128,1024]{2,1,0:T(8,128)(2,1)S(1)} %copy-done.7, bf16[1,128,1024]{2,1,0:T(8,128)(2,1)S(1)} %copy.77, ...), kind=kLoop, calls=%fused_computation.35 | loop fusion | flops 8912896 | bytes 5243904 | tf_op jit(solution)/shard_map/convert_element_type | solution.py:132
  (90 shorter events, 30.1 us)
Async XLA Ops:
  0.0 241.9 %copy-start = (bf16[1,384,4096]{2,1,0:T(8,128)(2,1)S(1)}, bf16[1,384,4096]{2,1,0:T(8,128)(2,1)}, u32[]{:S(2)}) copy-start(bf16[1,384,4096]{2,1,0:T(8,128)(2,1)} %param.15) | copy-start | bytes 9437188
  0.0 19.1 %copy-start.16 = (s32[1,128,2]{1,2,0:T(2,128)S(1)}, s32[1,128,2]{1,2,0:T(2,128)}, u32[]{:S(2)}) copy-start(s32[1,128,2]{1,2,0:T(2,128)} %param.13) | copy-start | bytes 3076
  14.4 16.0 %all-to-all-start = ((bf16[4,128,2,256]{3,1,2,0:T(8,128)(2,1)}), bf16[4,128,2,256]{3,1,2,0:T(8,128)(2,1)}, u32[]{:S(2)}, u32[]{:S(2)}) async-start(bf16[4,128,2,256]{3,1,2,0:T(8,128)(2,1)} %gather_fusion.1), calls=%async_computation | async-start | bytes 1048576 | tf_op jit(solution)/shard_map/all_to_all | solution.py:70
  32.8 2.8 copy-start.11
  33.9 9.1 %copy-start.14 = (bf16[384,256]{1,0:T(8,128)(2,1)}, bf16[384,256]{1,0:T(8,128)(2,1)S(1)}, u32[]{:S(2)}) copy-start(bf16[384,256]{1,0:T(8,128)(2,1)S(1)} %get-tuple-element.23) | copy-start | bytes 589828
  33.9 2.4 copy-start.10
  35.5 2.9 copy-start.2
  35.6 1.3 copy-start.6
  35.6 1.3 copy-start.12
  36.2 2.3 copy-start.3
  36.9 2.7 copy-start.1
  39.5 3.4 copy-start.13
  222.4 6.0 %collective-permute-start = (bf16[16,24,4096]{2,1,0:T(8,128)(2,1)}, bf16[16,24,4096]{2,1,0:T(8,128)(2,1)}, u32[]{:S(2)}, u32[]{:S(2)}) collective-permute-start(bf16[16,24,4096]{2,1,0:T(8,128)(2,1)} %all_to_all.15), channel_id=1, source_target_pairs={{0,1},{1,0},{2,3},{3,2},{4,5},{5,4},{6,7},{7,6},{8,9},{9,8},{10,11... | collective-permute-start | bytes 9437192 | tf_op jit(solution)/shard_map/ppermute | solution.py:16
  241.9 4.5 %copy-start.5 = (bf16[768,1,384]{2,0,1:T(8,128)(2,1)}, bf16[768,1,384]{2,0,1:T(8,128)(2,1)S(1)}, u32[]{:S(2)}) copy-start(bf16[768,1,384]{2,0,1:T(8,128)(2,1)S(1)} %fusion.27) | copy-start | bytes 1769476
  246.3 10.5 %collective-permute-start.1 = (f32[16,48,2048]{2,1,0:T(8,128)}, f32[16,48,2048]{2,1,0:T(8,128)}, u32[]{:S(2)}, u32[]{:S(2)}) collective-permute-start(f32[16,48,2048]{2,1,0:T(8,128)} %fusion.18), channel_id=1, source_target_pairs={{0,1},{1,0},{2,3},{3,2},{4,5},{5,4},{6,7},{7,6},{8,9},{9,8},{10,11... | collective-permute-start | bytes 18874376 | tf_op jit(solution)/shard_map/ppermute | solution.py:16
  263.3 5.6 %copy-start.15 = (bf16[4096,8]{0,1:T(8,128)(2,1)S(1)}, bf16[4096,8]{0,1:T(8,128)(2,1)}, u32[]{:S(2)}) copy-start(bf16[4096,8]{0,1:T(8,128)(2,1)} %param.12) | copy-start | bytes 196612
  263.3 75.2 %all-to-all-start.2 = ((bf16[16,48,2048]{2,1,0:T(8,128)(2,1)}), bf16[16,48,2048]{2,1,0:T(8,128)(2,1)}, u32[]{:S(2)}, u32[]{:S(2)}) async-start(bf16[16,48,2048]{2,1,0:T(8,128)(2,1)} %add_convert_fusion), calls=%async_computation.2 | async-start | bytes 6291456 | tf_op jit(solution)/shard_map/all_to_all | solution.py:122
  354.4 6.3 %copy-start.4 = (bf16[1,128,4096]{2,1,0:T(8,128)(2,1)S(1)}, bf16[1,128,4096]{2,1,0:T(8,128)(2,1)}, u32[]{:S(2)}) copy-start(bf16[1,128,4096]{2,1,0:T(8,128)(2,1)} %param.10) | copy-start | bytes 3145732
  354.4 6.3 %copy-start.7 = (bf16[1,128,1024]{2,1,0:T(8,128)(2,1)S(1)}, bf16[1,128,1024]{2,1,0:T(8,128)(2,1)}, u32[]{:S(2)}) copy-start(bf16[1,128,1024]{2,1,0:T(8,128)(2,1)} %copy.78) | copy-start | bytes 786436
  354.4 6.3 %copy-start.8 = (bf16[1,128,1024]{2,1,0:T(8,128)(2,1)S(1)}, bf16[1,128,1024]{2,1,0:T(8,128)(2,1)}, u32[]{:S(2)}) copy-start(bf16[1,128,1024]{2,1,0:T(8,128)(2,1)} %copy.79) | copy-start | bytes 786436
  354.4 6.3 %copy-start.9 = (bf16[1,128,1024]{2,1,0:T(8,128)(2,1)S(1)}, bf16[1,128,1024]{2,1,0:T(8,128)(2,1)}, u32[]{:S(2)}) copy-start(bf16[1,128,1024]{2,1,0:T(8,128)(2,1)} %copy.80) | copy-start | bytes 786436
where the time goes:
time: 373 us; the launch traced here: 366 us
  local copies, waits for them, and re-layouts  130 us (35%)
  blocking collectives  87 us (23%)
  waiting for transfers between devices  78.8 us (21%)
  matrix products  38.1 us (10%)
  other arithmetic  21 us (6%)
  starting transfers between devices  10.3 us (3%)
    all_to_all x1, blocking collectives, on_device(): lax.all_to_all(halved, ('branch', 'seq'), split_axis=0, concat_axis=0, ti...  79.2 us
    scatter x1, local copies, waits for them, and re-layouts, on_device(): jnp.zeros((experts, capacity, D), jnp.bfloat16).at[flat_ids, slot_of]  66.6 us
    all_to_all x1, waiting for transfers between devices, on_device(): lax.all_to_all(finished, ('branch', 'seq'), split_axis=0, concat_axis=0,...  59.8 us
    ppermute x2, waiting for transfers between devices, swapped(): return lax.ppermute(value, axis, pairs)  16.3 us
    dot_general x4, matrix products, attend_block(): jnp.einsum('gtk,kd->tgd', probs, value_head, preferred_element_type=jnp.f...  13.8 us
    all_gather x1, blocking collectives, on_device(): suffix_all = lax.all_gather(keyvals, 'seq', axis=1, tiled=True)[0]  7.73 us
    gather x1, local copies, waits for them, and re-layouts, on_device(): expert_out = out_table[flat_ids, slot_of].reshape(block_len, top_count, D)  7.47 us
  transfers between devices with their start and end apart: 4, of which 4 were waited for; matrix products, arithmetic and copies ran while one was open for 5% of the time, Pallas kernels for 0%

commit v1 on v0

--- a/solution.py
+++ b/solution.py
@@ -94,7 +94,20 @@
     )
     pair_half = me_block % 2
     halved = sendbuf.reshape(experts * 2, half_cap, D)
-    own_share = lax.all_to_all(halved, ("branch", "seq"), split_axis=0, concat_axis=0, tiled=True)
+    ways, here = (lax.axis_size(("branch", "seq")), lax.axis_index(("branch", "seq")))
+    width = halved.shape[0] // ways
+    shape = list(halved.shape)
+    shape[0] = width
+    height = shape[0]
+    shape[0] = height * ways
+    own_share = jnp.zeros(shape, halved.dtype)
+    for mask_2 in range(ways):
+        part = lax.dynamic_slice_in_dim(halved, (here ^ mask_2) * width, width, axis=0)
+        if mask_2:
+            part = lax.ppermute(part, ("branch", "seq"), [(d, d ^ mask_2) for d in range(ways)])
+        own_share = lax.dynamic_update_slice_in_dim(
+            own_share, part, (here ^ mask_2) * height, axis=0
+        )
     theirs = swapped(own_share, "seq", 0)
     rows_in = jnp.where(
         pair_half == 0,

time: 373 us -> 384 us (1.029)
  blocking collectives: 87 us -> 7.73 us
  starting transfers between devices: 10.3 us -> 55.2 us
  waiting for transfers between devices: 78.8 us -> 109 us
  local copies, waits for them, and re-layouts: 130 us -> 145 us
    all_to_all x1 -> x0, blocking collectives: 79.2 us -> none  [on_device(): lax.all_to_all(halved, ('branch', 'seq'), split_axis=0, concat_axis=0, ti...]
    ppermute x0 -> x15, starting transfers between devices: none -> 44.5 us  [on_device(): lax.ppermute(part, ('branch', 'seq'), [(d, d ^ mask_2) for d in range(way...]
    ppermute x0 -> x15, waiting for transfers between devices: none -> 31.2 us  [on_device(): lax.ppermute(part, ('branch', 'seq'), [(d, d ^ mask_2) for d in range(way...]
    dynamic_update_slice x0 -> x15, local copies, waits for them, and re-layouts: none -> 10.4 us  [on_device(): lax.dynamic_update_slice_in_dim(own_share, part, (here ^ mask_2) * height...]
  transfers between devices with their start and end apart: 4 -> 19, of which waited for: 4 -> 11; matrix products, arithmetic and copies ran while one was open for 5% -> 7% of each run, Pallas kernels for 0% -> 0%
where the time goes in v1:
time: 384 us; the launch traced here: 378 us
  local copies, waits for them, and re-layouts  145 us (38%)
  waiting for transfers between devices  109 us (28%)
  starting transfers between devices  55.2 us (14%)
  matrix products  38.1 us (10%)
  other arithmetic  21 us (5%)
  blocking collectives  7.73 us (2%)
    scatter x1, local copies, waits for them, and re-layouts, on_device(): jnp.zeros((experts, capacity, D), jnp.bfloat16).at[flat_ids, slot_of]  67.4 us
    all_to_all x1, waiting for transfers between devices, on_device(): lax.all_to_all(finished, ('branch', 'seq'), split_axis=0, concat_axis=0,...  59.8 us
    ppermute x15, starting transfers between devices, on_device(): lax.ppermute(part, ('branch', 'seq'), [(d, d ^ mask_2) for d in range(way...  44.5 us
    ppermute x15, waiting for transfers between devices, on_device(): lax.ppermute(part, ('branch', 'seq'), [(d, d ^ mask_2) for d in range(way...  31.2 us
    ppermute x2, waiting for transfers between devices, swapped(): return lax.ppermute(value, axis, pairs)  15.8 us
    dot_general x4, matrix products, attend_block(): jnp.einsum('gtk,kd->tgd', probs, value_head, preferred_element_type=jnp.f...  13.9 us
    dynamic_update_slice x15, local copies, waits for them, and re-layouts, on_device(): lax.dynamic_update_slice_in_dim(own_share, part, (here ^ mask_2) * height...  10.4 us
    all_gather x1, blocking collectives, on_device(): suffix_all = lax.all_gather(keyvals, 'seq', axis=1, tiled=True)[0]  7.73 us
  transfers between devices with their start and end apart: 19, of which 11 were waited for; matrix products, arithmetic and copies ran while one was open for 7% of the time, Pallas kernels for 0%

profile of v1, /device:TPU:11, one launch (start us, length us, event | category | flops | bytes accessed | tf_op | source)
XLA Modules:
  0.0 377.6 jit_solution(5710029859823294218)
XLA Ops:
  1.1 7.7 %all_gather.3 = bf16[1,512,2,256]{3,1,2,0:T(8,128)(2,1)} all-gather(bf16[1,128,2,256]{3,1,2,0:T(8,128)(2,1)S(1)} %copy.62), channel_id=1, replica_groups=mesh['rollout'=2,'branch'=4,'seq'=4] {'seq'}, dimensions={1}, use_global_device_ids=true | all-gather | bytes 655360 | tf_op jit(solution)/shard_map/all_gather | solution.py:62
  14.4 4.8 %all-to-all-start = ((bf16[4,128,2,256]{3,1,2,0:T(8,128)(2,1)}), bf16[4,128,2,256]{3,1,2,0:T(8,128)(2,1)}, u32[]{:S(2)}, u32[]{:S(2)}) async-start(bf16[4,128,2,256]{3,1,2,0:T(8,128)(2,1)} %gather_fusion.1), calls=%async_computation | async-start | bytes 1048576 | tf_op jit(solution)/shard_map/all_to_all | solution.py:70
  39.5 3.4 fusion.6
  45.8 4.0 %fusion.25 = bf16[128,8,128]{2,0,1:T(8,128)(2,1)} fusion(f32[896,128,8]{1,0,2:T(8,128)} %copy-done.4, f32[8,128]{1,0:T(8,128)S(1)} %get-tuple-element.6, f32[8,128]{1,0:T(8,128)S(1)} %get-tuple-element.47, pred[128,896]{0,1:T(8,128)(4,1)} %concatenate.44, bf16[512,256]{1,0:T(8,128)(2,1)} %get-tuple-element.37, bf16[384,256]{1,0:T(8,128)(2,1)} %copy-done.15), kind=kOutput, calls=%fused_computation.52 | convolution fusion | flops 240058368 | bytes 4513792 | tf_op jit(solution)/shard_map/gtk,kd->tgd/dot_general | solution.py:48
  51.6 4.0 %fusion.24 = bf16[128,8,128]{2,0,1:T(8,128)(2,1)} fusion(f32[896,128,8]{1,0,2:T(8,128)} %copy-done.3, f32[8,128]{1,0:T(8,128)S(1)} %get-tuple-element.7, f32[8,128]{1,0:T(8,128)S(1)} %get-tuple-element.46, pred[128,896]{0,1:T(8,128)(4,1)} %concatenate.44, bf16[384,256]{1,0:T(8,128)(2,1)} %copy-done.15, bf16[512,256]{1,0:T(8,128)(2,1)} %get-tuple-element.37), kind=kOutput, calls=%fused_computation.51 | convolution fusion | flops 240058368 | bytes 4513792 | tf_op jit(solution)/shard_map/gtk,kd->tgd/dot_general | solution.py:48
  57.4 4.0 %fusion.23 = bf16[128,8,128]{2,0,1:T(8,128)(2,1)} fusion(f32[896,128,8]{1,0,2:T(8,128)} %copy-done.2, f32[8,128]{1,0:T(8,128)S(1)} %get-tuple-element.8, f32[8,128]{1,0:T(8,128)S(1)} %get-tuple-element.45, pred[128,896]{0,1:T(8,128)(4,1)} %concatenate.44, bf16[384,256]{1,0:T(8,128)(2,1)} %copy-done.15, bf16[512,256]{1,0:T(8,128)(2,1)} %get-tuple-element.37), kind=kOutput, calls=%fused_computation.50 | convolution fusion | flops 240058368 | bytes 4513792 | tf_op jit(solution)/shard_map/gtk,kd->tgd/dot_general | solution.py:48
  65.1 2.8 multiply_convert_fusion
  67.9 6.6 %gather_fusion.3 = bf16[256,4096]{1,0:T(8,128)(2,1)} fusion(bf16[128,4096]{1,0:T(8,128)(2,1)} %multiply_convert_fusion, s32[1024]{0:T(1024)S(1)} %pad_clamp_fusion), kind=kCustom, calls=%fused_computation.3 | custom fusion | bytes 4195328 | tf_op jit(solution)/shard_map/gather | solution.py:93
  76.5 67.4 %scatter_fusion = bf16[8,48,4096]{2,1,0:T(8,128)(2,1)} fusion(bf16[8,48,4096]{2,1,0:T(8,128)(2,1)} %broadcast_in_dim.36, s32[256]{0:T(256)S(1)} %bitcast.187, bf16[256,4096]{1,0:T(8,128)(2,1)} %gather_fusion.3), kind=kCustom, calls=%fused_computation.6 | custom fusion | bytes 6293504 | tf_op jit(solution)/shard_map/scatter | solution.py:93
  151.4 3.0 collective-permute-start.3
  156.7 3.7 collective-permute-start.6
  164.8 3.5 collective-permute-start.9
  169.0 3.4 collective-permute-done.5
  172.4 6.4 %collective-permute-start.10 = (bf16[1,24,4096]{2,1,0:T(8,128)(2,1)S(1)}, bf16[1,24,4096]{2,1,0:T(8,128)(2,1)S(1)}, u32[]{:S(2)}, u32[]{:S(2)}) collective-permute-start(bf16[1,24,4096]{2,1,0:T(8,128)(2,1)S(1)} %get-tuple-element.19), channel_id=1, source_target_pairs={{0,11},{1,10},{2,9},{3,8},{4,15},{5,14},{6,13},{7,12},{8,3},{9,2},... | collective-permute-start | bytes 589832 | tf_op jit(solution)/shard_map/ppermute | solution.py:107
  181.2 17.7 %collective-permute-start.13 = (bf16[1,24,4096]{2,1,0:T(8,128)(2,1)S(1)}, bf16[1,24,4096]{2,1,0:T(8,128)(2,1)S(1)}, u32[]{:S(2)}, u32[]{:S(2)}) collective-permute-start(bf16[1,24,4096]{2,1,0:T(8,128)(2,1)S(1)} %get-tuple-element.16), channel_id=1, source_target_pairs={{0,14},{1,15},{2,12},{3,13},{4,10},{5,11},{6,8},{7,9},{8,6},{9,7},... | collective-permute-start | bytes 589832 | tf_op jit(solution)/shard_map/ppermute | solution.py:107
  204.5 9.4 %collective-permute-done.10 = bf16[1,24,4096]{2,1,0:T(8,128)(2,1)S(1)} collective-permute-done((bf16[1,24,4096]{2,1,0:T(8,128)(2,1)S(1)}, bf16[1,24,4096]{2,1,0:T(8,128)(2,1)S(1)}, u32[]{:S(2)}, u32[]{:S(2)}) %collective-permute-start.10) | collective-permute-done | bytes 196640 | tf_op jit(solution)/shard_map/ppermute | solution.py:107
  214.6 6.1 %collective-permute-done.11 = bf16[1,24,4096]{2,1,0:T(8,128)(2,1)S(1)} collective-permute-done((bf16[1,24,4096]{2,1,0:T(8,128)(2,1)S(1)}, bf16[1,24,4096]{2,1,0:T(8,128)(2,1)S(1)}, u32[]{:S(2)}, u32[]{:S(2)}) %collective-permute-start.11) | collective-permute-done | bytes 196640 | tf_op jit(solution)/shard_map/ppermute | solution.py:107
  221.5 4.3 %collective-permute-done.12 = bf16[1,24,4096]{2,1,0:T(8,128)(2,1)S(1)} collective-permute-done((bf16[1,24,4096]{2,1,0:T(8,128)(2,1)S(1)}, bf16[1,24,4096]{2,1,0:T(8,128)(2,1)S(1)}, u32[]{:S(2)}, u32[]{:S(2)}) %collective-permute-start.12) | collective-permute-done | bytes 196640 | tf_op jit(solution)/shard_map/ppermute | solution.py:107
  229.8 3.5 collective-permute-done.14
  234.4 5.6 %collective-permute-done.15 = bf16[16,24,4096]{2,1,0:T(8,128)(2,1)} collective-permute-done((bf16[16,24,4096]{2,1,0:T(8,128)(2,1)}, bf16[16,24,4096]{2,1,0:T(8,128)(2,1)}, u32[]{:S(2)}, u32[]{:S(2)}) %collective-permute-start.15) | collective-permute-done | bytes 3145760 | tf_op jit(solution)/shard_map/ppermute | solution.py:16
  240.0 5.9 %maximum_select_fusion = bf16[16,48,4096]{2,1,0:T(8,128)(2,1)S(1)} fusion(bf16[16,24,4096]{2,1,0:T(8,128)(2,1)} %collective-permute-done.15, bf16[16,24,4096]{2,1,0:T(8,128)(2,1)} %constant_dynamic-update-slice_fusion, pred[]{:T(512)S(6)} %eq.34), kind=kLoop, calls=%fused_computation.7 | loop fusion | flops 28311552 | bytes 12582913 | tf_op jit(solution)/shard_map/jit(_where)/select_n | solution.py:112
  245.9 7.3 %fusion = f32[768,2,384]{2,0,1:T(8,128)S(1)} fusion(bf16[768,4096,1]{1,0,2:T(8,128)(2,1)S(1)} %bitcast.190, bf16[4096,2,384]{2,1,0:T(2,128)(2,1)} %bitcast.209), kind=kOutput, calls=%fused_computation.8 | convolution fusion | flops 4831838208 | bytes 14942208 | tf_op jit(solution)/shard_map/rd,dcf->rcf/dot_general | solution.py:120
  253.6 4.5 %fusion.18 = f32[16,48,2048]{2,1,0:T(8,128)} fusion(bf16[16,48,384]{2,1,0:T(8,128)(2,1)S(1)} %bitcast.188, bf16[1,384,4096]{2,1,0:T(8,128)(2,1)S(1)} %copy-done, s32[]{:T(128)S(6)} %select_n.279), kind=kOutput, calls=%fused_computation.45 | convolution fusion | flops 1207959552 | bytes 8454148 | tf_op jit(solution)/shard_map/dot_general | solution.py:130
  258.4 10.1 %collective-permute-done.16 = f32[16,48,2048]{2,1,0:T(8,128)} collective-permute-done((f32[16,48,2048]{2,1,0:T(8,128)}, f32[16,48,2048]{2,1,0:T(8,128)}, u32[]{:S(2)}, u32[]{:S(2)}) %collective-permute-start.16) | collective-permute-done | bytes 6291488 | tf_op jit(solution)/shard_map/ppermute | solution.py:16
  268.5 6.5 %add_convert_fusion = bf16[16,48,2048]{2,1,0:T(8,128)(2,1)} fusion(f32[16,48,2048]{2,1,0:T(8,128)} %collective-permute-done.16, bf16[16,48,384]{2,1,0:T(8,128)(2,1)} %bitcast.189, bf16[1,384,4096]{2,1,0:T(8,128)(2,1)S(1)} %copy-done, s32[]{:T(128)S(6)} %select_n.278), kind=kOutput, calls=%fused_computation.10 | convolution fusion | flops 1211105280 | bytes 11599876 | tf_op jit(solution)/shard_map/dot_general | solution.py:127
  275.0 5.2 %all-to-all-start.1 = ((bf16[16,48,2048]{2,1,0:T(8,128)(2,1)}), bf16[16,48,2048]{2,1,0:T(8,128)(2,1)}, u32[]{:S(2)}, u32[]{:S(2)}) async-start(bf16[16,48,2048]{2,1,0:T(8,128)(2,1)} %add_convert_fusion), calls=%async_computation.1 | async-start | bytes 6291456 | tf_op jit(solution)/shard_map/all_to_all | solution.py:135
  290.2 59.8 %all-to-all-done.1 = bf16[16,48,2048]{2,1,0:T(8,128)(2,1)} async-done(((bf16[16,48,2048]{2,1,0:T(8,128)(2,1)}), bf16[16,48,2048]{2,1,0:T(8,128)(2,1)}, u32[]{:S(2)}, u32[]{:S(2)}) %all-to-all-start.1) | async-done | bytes 3145760 | tf_op jit(solution)/shard_map/all_to_all | solution.py:135
  350.1 4.0 %copy.114 = bf16[8,2,6,8,2048]{4,3,1,2,0:T(8,128)(2,1)} copy(bf16[8,2,6,8,2048]{4,3,2,1,0:T(8,128)(2,1)} %bitcast.75) | data formatting | bytes 6291456 | tf_op jit(solution)/shard_map/reshape | solution.py:136
  354.0 7.5 %gather_fusion.4 = bf16[256,4096]{1,0:T(8,128)(2,1)} fusion(bf16[8,48,4096]{2,1,0:T(8,128)(2,1)} %bitcast.185, s32[256]{0:T(256)S(1)} %bitcast.186), kind=kCustom, calls=%fused_computation.4 | custom fusion | bytes 4196352 | tf_op jit(solution)/shard_map/gather | solution.py:139
  361.5 4.4 %reshape.546 = bf16[128,2,4096]{2,1,0:T(2,128)(2,1)} reshape(bf16[256,4096]{1,0:T(8,128)(2,1)} %gather_fusion.4) | data formatting | bytes 4194304 | tf_op jit(solution)/shard_map/reshape | solution.py:139
  365.9 6.1 %fusion.76 = (bf16[128,1,4096]{2,1,0:T(2,128)(2,1)S(1)}, bf16[128,1,4096]{2,1,0:T(2,128)(2,1)S(1)}) fusion(bf16[128,2,4096]{2,1,0:T(2,128)(2,1)} %reshape.546), kind=kLoop, calls=%fused_computation.180 | loop fusion | bytes 4194304 | tf_op jit(solution)/shard_map/slice | solution.py:142
  372.1 5.2 %fusion.12 = bf16[1,128,4096]{2,1,0:T(8,128)(2,1)} fusion(bf16[1,128,4096]{2,1,0:T(8,128)(2,1)S(1)} %copy-done.5, bf16[1,128,1024]{2,1,0:T(8,128)(2,1)S(1)} %copy-done.10, bf16[1,128,1024]{2,1,0:T(8,128)(2,1)S(1)} %copy-done.9, bf16[1,128,1024]{2,1,0:T(8,128)(2,1)S(1)} %copy-done.8, bf16[1,128,1024]{2,1,0:T(8,128)(2,1)S(1)} %copy.77, ...), kind=kLoop, calls=%fused_computation.35 | loop fusion | flops 8912896 | bytes 5243904 | tf_op jit(solution)/shard_map/convert_element_type | solution.py:145
  (137 shorter events, 79.0 us)
Async XLA Ops:
  0.0 253.6 %copy-start = (bf16[1,384,4096]{2,1,0:T(8,128)(2,1)S(1)}, bf16[1,384,4096]{2,1,0:T(8,128)(2,1)}, u32[]{:S(2)}) copy-start(bf16[1,384,4096]{2,1,0:T(8,128)(2,1)} %param.15) | copy-start | bytes 9437188
  0.0 19.1 %copy-start.17 = (s32[1,128,2]{1,2,0:T(2,128)S(1)}, s32[1,128,2]{1,2,0:T(2,128)}, u32[]{:S(2)}) copy-start(s32[1,128,2]{1,2,0:T(2,128)} %param.13) | copy-start | bytes 3076
  14.4 16.0 %all-to-all-start = ((bf16[4,128,2,256]{3,1,2,0:T(8,128)(2,1)}), bf16[4,128,2,256]{3,1,2,0:T(8,128)(2,1)}, u32[]{:S(2)}, u32[]{:S(2)}) async-start(bf16[4,128,2,256]{3,1,2,0:T(8,128)(2,1)} %gather_fusion.1), calls=%async_computation | async-start | bytes 1048576 | tf_op jit(solution)/shard_map/all_to_all | solution.py:70
  33.8 9.1 %copy-start.15 = (bf16[384,256]{1,0:T(8,128)(2,1)}, bf16[384,256]{1,0:T(8,128)(2,1)S(1)}, u32[]{:S(2)}) copy-start(bf16[384,256]{1,0:T(8,128)(2,1)S(1)} %get-tuple-element.39) | copy-start | bytes 589828
  35.5 3.5 copy-start.3
  36.2 2.8 copy-start.4
  39.5 3.4 copy-start.14
  143.8 3.0 copy-start.1
  147.9 6.6 %collective-permute-start = (bf16[1,24,4096]{2,1,0:T(8,128)(2,1)S(1)}, bf16[1,24,4096]{2,1,0:T(8,128)(2,1)S(1)}, u32[]{:S(2)}, u32[]{:S(2)}) collective-permute-start(bf16[1,24,4096]{2,1,0:T(8,128)(2,1)S(1)} %get-tuple-element.29), channel_id=1, source_target_pairs={{0,1},{1,0},{2,3},{3,2},{4,5},{5,4},{6,7},{7,6},{8,9},{9,8},{10,11... | collective-permute-start | bytes 589832 | tf_op jit(solution)/shard_map/ppermute | solution.py:107
  149.8 6.9 %collective-permute-start.1 = (bf16[1,24,4096]{2,1,0:T(8,128)(2,1)S(1)}, bf16[1,24,4096]{2,1,0:T(8,128)(2,1)S(1)}, u32[]{:S(2)}, u32[]{:S(2)}) collective-permute-start(bf16[1,24,4096]{2,1,0:T(8,128)(2,1)S(1)} %get-tuple-element.28), channel_id=1, source_target_pairs={{0,2},{1,3},{2,0},{3,1},{4,6},{5,7},{6,4},{7,5},{8,10},{9,11},{10,... | collective-permute-start | bytes 589832 | tf_op jit(solution)/shard_map/ppermute | solution.py:107
  150.2 10.8 %collective-permute-start.2 = (bf16[1,24,4096]{2,1,0:T(8,128)(2,1)S(1)}, bf16[1,24,4096]{2,1,0:T(8,128)(2,1)S(1)}, u32[]{:S(2)}, u32[]{:S(2)}) collective-permute-start(bf16[1,24,4096]{2,1,0:T(8,128)(2,1)S(1)} %get-tuple-element.27), channel_id=1, source_target_pairs={{0,3},{1,2},{2,1},{3,0},{4,7},{5,6},{6,5},{7,4},{8,11},{9,10},{10,... | collective-permute-start | bytes 589832 | tf_op jit(solution)/shard_map/ppermute | solution.py:107
  151.4 12.5 %collective-permute-start.3 = (bf16[1,24,4096]{2,1,0:T(8,128)(2,1)S(1)}, bf16[1,24,4096]{2,1,0:T(8,128)(2,1)S(1)}, u32[]{:S(2)}, u32[]{:S(2)}) collective-permute-start(bf16[1,24,4096]{2,1,0:T(8,128)(2,1)S(1)} %get-tuple-element.26), channel_id=1, source_target_pairs={{0,4},{1,5},{2,6},{3,7},{4,0},{5,1},{6,2},{7,3},{8,12},{9,13},{10,... | collective-permute-start | bytes 589832 | tf_op jit(solution)/shard_map/ppermute | solution.py:107
  154.4 10.4 %collective-permute-start.4 = (bf16[1,24,4096]{2,1,0:T(8,128)(2,1)S(1)}, bf16[1,24,4096]{2,1,0:T(8,128)(2,1)S(1)}, u32[]{:S(2)}, u32[]{:S(2)}) collective-permute-start(bf16[1,24,4096]{2,1,0:T(8,128)(2,1)S(1)} %get-tuple-element.25), channel_id=1, source_target_pairs={{0,5},{1,4},{2,7},{3,6},{4,1},{5,0},{6,3},{7,2},{8,13},{9,12},{10,... | collective-permute-start | bytes 589832 | tf_op jit(solution)/shard_map/ppermute | solution.py:107
  154.5 17.9 %collective-permute-start.5 = (bf16[1,24,4096]{2,1,0:T(8,128)(2,1)S(1)}, bf16[1,24,4096]{2,1,0:T(8,128)(2,1)S(1)}, u32[]{:S(2)}, u32[]{:S(2)}) collective-permute-start(bf16[1,24,4096]{2,1,0:T(8,128)(2,1)S(1)} %get-tuple-element.24), channel_id=1, source_target_pairs={{0,6},{1,7},{2,4},{3,5},{4,2},{5,3},{6,0},{7,1},{8,14},{9,15},{10,... | collective-permute-start | bytes 589832 | tf_op jit(solution)/shard_map/ppermute | solution.py:107
  156.7 22.8 %collective-permute-start.6 = (bf16[1,24,4096]{2,1,0:T(8,128)(2,1)S(1)}, bf16[1,24,4096]{2,1,0:T(8,128)(2,1)S(1)}, u32[]{:S(2)}, u32[]{:S(2)}) collective-permute-start(bf16[1,24,4096]{2,1,0:T(8,128)(2,1)S(1)} %get-tuple-element.23), channel_id=1, source_target_pairs={{0,7},{1,6},{2,5},{3,4},{4,3},{5,2},{6,1},{7,0},{8,15},{9,14},{10,... | collective-permute-start | bytes 589832 | tf_op jit(solution)/shard_map/ppermute | solution.py:107
  161.0 19.1 %collective-permute-start.7 = (bf16[1,24,4096]{2,1,0:T(8,128)(2,1)S(1)}, bf16[1,24,4096]{2,1,0:T(8,128)(2,1)S(1)}, u32[]{:S(2)}, u32[]{:S(2)}) collective-permute-start(bf16[1,24,4096]{2,1,0:T(8,128)(2,1)S(1)} %get-tuple-element.22), channel_id=1, source_target_pairs={{0,8},{1,9},{2,10},{3,11},{4,12},{5,13},{6,14},{7,15},{8,0},{9,1},... | collective-permute-start | bytes 589832 | tf_op jit(solution)/shard_map/ppermute | solution.py:107
  163.9 17.3 %collective-permute-start.8 = (bf16[1,24,4096]{2,1,0:T(8,128)(2,1)S(1)}, bf16[1,24,4096]{2,1,0:T(8,128)(2,1)S(1)}, u32[]{:S(2)}, u32[]{:S(2)}) collective-permute-start(bf16[1,24,4096]{2,1,0:T(8,128)(2,1)S(1)} %get-tuple-element.21), channel_id=1, source_target_pairs={{0,9},{1,8},{2,11},{3,10},{4,13},{5,12},{6,15},{7,14},{8,1},{9,0},... | collective-permute-start | bytes 589832 | tf_op jit(solution)/shard_map/ppermute | solution.py:107
  164.8 36.5 %collective-permute-start.9 = (bf16[1,24,4096]{2,1,0:T(8,128)(2,1)S(1)}, bf16[1,24,4096]{2,1,0:T(8,128)(2,1)S(1)}, u32[]{:S(2)}, u32[]{:S(2)}) collective-permute-start(bf16[1,24,4096]{2,1,0:T(8,128)(2,1)S(1)} %get-tuple-element.20), channel_id=1, source_target_pairs={{0,10},{1,11},{2,8},{3,9},{4,14},{5,15},{6,12},{7,13},{8,2},{9,3},... | collective-permute-start | bytes 589832 | tf_op jit(solution)/shard_map/ppermute | solution.py:107
  172.4 41.5 %collective-permute-start.10 = (bf16[1,24,4096]{2,1,0:T(8,128)(2,1)S(1)}, bf16[1,24,4096]{2,1,0:T(8,128)(2,1)S(1)}, u32[]{:S(2)}, u32[]{:S(2)}) collective-permute-start(bf16[1,24,4096]{2,1,0:T(8,128)(2,1)S(1)} %get-tuple-element.19), channel_id=1, source_target_pairs={{0,11},{1,10},{2,9},{3,8},{4,15},{5,14},{6,13},{7,12},{8,3},{9,2},... | collective-permute-start | bytes 589832 | tf_op jit(solution)/shard_map/ppermute | solution.py:107
  179.5 41.3 %collective-permute-start.11 = (bf16[1,24,4096]{2,1,0:T(8,128)(2,1)S(1)}, bf16[1,24,4096]{2,1,0:T(8,128)(2,1)S(1)}, u32[]{:S(2)}, u32[]{:S(2)}) collective-permute-start(bf16[1,24,4096]{2,1,0:T(8,128)(2,1)S(1)} %get-tuple-element.18), channel_id=1, source_target_pairs={{0,12},{1,13},{2,14},{3,15},{4,8},{5,9},{6,10},{7,11},{8,4},{9,5},... | collective-permute-start | bytes 589832 | tf_op jit(solution)/shard_map/ppermute | solution.py:107
  180.1 45.6 %collective-permute-start.12 = (bf16[1,24,4096]{2,1,0:T(8,128)(2,1)S(1)}, bf16[1,24,4096]{2,1,0:T(8,128)(2,1)S(1)}, u32[]{:S(2)}, u32[]{:S(2)}) collective-permute-start(bf16[1,24,4096]{2,1,0:T(8,128)(2,1)S(1)} %get-tuple-element.17), channel_id=1, source_target_pairs={{0,13},{1,12},{2,15},{3,14},{4,9},{5,8},{6,11},{7,10},{8,5},{9,4},... | collective-permute-start | bytes 589832 | tf_op jit(solution)/shard_map/ppermute | solution.py:107
  181.2 47.9 %collective-permute-start.13 = (bf16[1,24,4096]{2,1,0:T(8,128)(2,1)S(1)}, bf16[1,24,4096]{2,1,0:T(8,128)(2,1)S(1)}, u32[]{:S(2)}, u32[]{:S(2)}) collective-permute-start(bf16[1,24,4096]{2,1,0:T(8,128)(2,1)S(1)} %get-tuple-element.16), channel_id=1, source_target_pairs={{0,14},{1,15},{2,12},{3,13},{4,10},{5,11},{6,8},{7,9},{8,6},{9,7},... | collective-permute-start | bytes 589832 | tf_op jit(solution)/shard_map/ppermute | solution.py:107
  201.3 32.0 %collective-permute-start.14 = (bf16[1,24,4096]{2,1,0:T(8,128)(2,1)S(1)}, bf16[1,24,4096]{2,1,0:T(8,128)(2,1)S(1)}, u32[]{:S(2)}, u32[]{:S(2)}) collective-permute-start(bf16[1,24,4096]{2,1,0:T(8,128)(2,1)S(1)} %get-tuple-element.15), channel_id=1, source_target_pairs={{0,15},{1,14},{2,13},{3,12},{4,11},{5,10},{6,9},{7,8},{8,7},{9,6},... | collective-permute-start | bytes 589832 | tf_op jit(solution)/shard_map/ppermute | solution.py:107
  234.0 6.0 %collective-permute-start.15 = (bf16[16,24,4096]{2,1,0:T(8,128)(2,1)}, bf16[16,24,4096]{2,1,0:T(8,128)(2,1)}, u32[]{:S(2)}, u32[]{:S(2)}) collective-permute-start(bf16[16,24,4096]{2,1,0:T(8,128)(2,1)} %constant_dynamic-update-slice_fusion), channel_id=1, source_target_pairs={{0,1},{1,0},{2,3},{3,2},{4,5},{5,4},{6,7},{7,6},{8,9},{9,8},{10,11... | collective-permute-start | bytes 9437192 | tf_op jit(solution)/shard_map/ppermute | solution.py:16
  253.5 4.5 %copy-start.6 = (bf16[768,1,384]{2,0,1:T(8,128)(2,1)}, bf16[768,1,384]{2,0,1:T(8,128)(2,1)S(1)}, u32[]{:S(2)}) copy-start(bf16[768,1,384]{2,0,1:T(8,128)(2,1)S(1)} %fusion.27) | copy-start | bytes 1769476
  258.0 10.5 %collective-permute-start.16 = (f32[16,48,2048]{2,1,0:T(8,128)}, f32[16,48,2048]{2,1,0:T(8,128)}, u32[]{:S(2)}, u32[]{:S(2)}) collective-permute-start(f32[16,48,2048]{2,1,0:T(8,128)} %fusion.18), channel_id=1, source_target_pairs={{0,1},{1,0},{2,3},{3,2},{4,5},{5,4},{6,7},{7,6},{8,9},{9,8},{10,11... | collective-permute-start | bytes 18874376 | tf_op jit(solution)/shard_map/ppermute | solution.py:16
  275.0 5.5 %copy-start.16 = (bf16[4096,8]{0,1:T(8,128)(2,1)S(1)}, bf16[4096,8]{0,1:T(8,128)(2,1)}, u32[]{:S(2)}) copy-start(bf16[4096,8]{0,1:T(8,128)(2,1)} %param.12) | copy-start | bytes 196612
  275.0 75.0 %all-to-all-start.1 = ((bf16[16,48,2048]{2,1,0:T(8,128)(2,1)}), bf16[16,48,2048]{2,1,0:T(8,128)(2,1)}, u32[]{:S(2)}, u32[]{:S(2)}) async-start(bf16[16,48,2048]{2,1,0:T(8,128)(2,1)} %add_convert_fusion), calls=%async_computation.1 | async-start | bytes 6291456 | tf_op jit(solution)/shard_map/all_to_all | solution.py:135
  365.9 6.1 %copy-start.5 = (bf16[1,128,4096]{2,1,0:T(8,128)(2,1)S(1)}, bf16[1,128,4096]{2,1,0:T(8,128)(2,1)}, u32[]{:S(2)}) copy-start(bf16[1,128,4096]{2,1,0:T(8,128)(2,1)} %param.10) | copy-start | bytes 3145732
  365.9 6.1 %copy-start.8 = (bf16[1,128,1024]{2,1,0:T(8,128)(2,1)S(1)}, bf16[1,128,1024]{2,1,0:T(8,128)(2,1)}, u32[]{:S(2)}) copy-start(bf16[1,128,1024]{2,1,0:T(8,128)(2,1)} %copy.78) | copy-start | bytes 786436
  365.9 6.2 %copy-start.9 = (bf16[1,128,1024]{2,1,0:T(8,128)(2,1)S(1)}, bf16[1,128,1024]{2,1,0:T(8,128)(2,1)}, u32[]{:S(2)}) copy-start(bf16[1,128,1024]{2,1,0:T(8,128)(2,1)} %copy.79) | copy-start | bytes 786436
  365.9 6.2 %copy-start.10 = (bf16[1,128,1024]{2,1,0:T(8,128)(2,1)S(1)}, bf16[1,128,1024]{2,1,0:T(8,128)(2,1)}, u32[]{:S(2)}) copy-start(bf16[1,128,1024]{2,1,0:T(8,128)(2,1)} %copy.80) | copy-start | bytes 786436
  (5 other events, 8.6 us)
